TPU v7x, 128 devices: a whole 4x4x4 slice. The times are simulated.
128 devices in a mesh: state: 32 (over x, y, core), mem: 4 (over z).
Axes of the slice: x: 4, y: 4, z: 4, core: 2. Of those that a mesh axis runs over, the one named last changes fastest.
Arguments:
- ensemble: bfloat16 [80, 1048576], P('mem', 'state'), may hold values from -6 to 6
- weights: bfloat16 [8192, 12, 128], P('state'), may hold values from 0 to 0.14941406
- seg_obs: int32 [8192, 12], P('state'), may hold values from 0 to 65535, as said below
- observed: float32 [65536], replicated, may hold values from -180 to 180
- inv_var: float32 [65536], replicated, may hold values from 0.0001 to 0.001
Outputs:
- analysis: bfloat16 [80, 1048576], P('mem', 'state')
Inputs may be any that keep to these rules, and one draw needn't show every extreme that they name: seg_obs names the observation that a slot's arc segment contributes to. Of the 3072 slots of the tiles of one index of state, exactly 96 name observations in each aligned block of 2048 observations; an observation may have any number of slots, or none.
All inputs are finite; a program needn't handle non-finite values.
Results may differ from a plain program's by a relative error of at most 0.0051.
Values may be sent and summed in bfloat16 or wider, within the bound.
A program may use at most 128 MiB of HBM per device.

v0:
```python
import math
import jax
import jax.numpy as jnp
from jax import lax
from jax.sharding import PartitionSpec as P

ITERS = 14


def sent_together(arrays, axis, split_dim, concat_dim, along):
    widths = [math.prod(a.shape[along:]) for a in arrays]
    both = jnp.concatenate(
        [a.reshape(*a.shape[:along], w) for a, w in zip(arrays, widths)], axis=along
    )
    out = lax.all_to_all(both, axis, split_axis=split_dim, concat_axis=concat_dim, tiled=True)
    parts = jnp.split(out, [sum(widths[:k]) for k in range(1, len(widths))], axis=along)
    return tuple((b.reshape(*out.shape[:along], *a.shape[along:]) for a, b in zip(arrays, parts)))


def copy_for_each(x, axis):
    peers = lax.axis_size(axis)
    return lax.all_to_all(jnp.broadcast_to(x[None], (peers, *x.shape)), axis, 0, 0, tiled=True)


def taken_together(x, axis):
    everything = copy_for_each(x, axis)
    return jnp.sum(everything, axis=0)


def in_one(arrays, axis):
    ends = [0]
    for a in arrays:
        ends.append(ends[-1] + a.size)
    subtotal = taken_together(jnp.concatenate([a.ravel() for a in arrays]), axis)
    return tuple((subtotal[b:e].reshape(a.shape) for a, b, e in zip(arrays, ends, ends[1:])))


def transform(gram, pull, members):
    identity = jnp.eye(members, dtype=jnp.float32)
    system = (members - 1.0) * identity + gram
    scaling = jnp.sqrt(jnp.sum(system * system))
    ynow = system / scaling
    znow = identity
    for step in range(ITERS):
        correct = 1.5 * identity - 0.5 * jnp.dot(znow, ynow, precision=lax.Precision.HIGHEST)
        ynow = jnp.dot(ynow, correct, precision=lax.Precision.HIGHEST)
        znow = jnp.dot(correct, znow, precision=lax.Precision.HIGHEST)
    root = znow / jnp.sqrt(scaling)
    shift = jnp.dot(
        root, jnp.dot(root, pull, precision=lax.Precision.HIGHEST), precision=lax.Precision.HIGHEST
    )
    mixed = shift[:, None] + math.sqrt(members - 1.0) * root
    mixed = mixed + (1.0 - jnp.sum(mixed, axis=0, keepdims=True)) / members
    return mixed.astype(jnp.bfloat16)


def statistics(everyone, obs_here, var_here, members):
    mean_obs = jnp.sum(everyone, axis=0) / members
    anomaly = everyone - mean_obs
    weighted = anomaly * var_here
    gram = jnp.dot(weighted, anomaly.T, precision=lax.Precision.HIGHEST)
    pull = jnp.dot(weighted, obs_here - mean_obs, precision=lax.Precision.HIGHEST)
    return (gram, pull)


def gather_members(shares):
    return lax.all_gather(shares.astype(jnp.bfloat16), "mem", axis=0, tiled=True).astype(
        jnp.float32
    )


def per_device(ensemble, weights, seg_obs, observed, inv_var):
    own_members, own_cells = ensemble.shape
    own_tiles, own_slots, tile_width = weights.shape
    obs_count = observed.shape[0]
    all_members = own_members * lax.axis_size("mem")
    blocks = ensemble.reshape(own_members, own_tiles, tile_width)
    values = jnp.einsum("ktc,tjc->tjk", blocks, weights, preferred_element_type=jnp.float32)
    values = values.reshape(own_tiles * own_slots, own_members)
    slot_ids = seg_obs.reshape(-1)
    share_width = obs_count // lax.axis_size("state")
    owner = slot_ids // share_width
    order = jnp.argsort(owner, stable=True)
    sorted_values = values[order]
    local_place = (slot_ids[order] % share_width).astype(jnp.float32)
    arrived, arrived_place = sent_together((sorted_values, local_place), "state", 0, 0, 1)
    landed = jax.ops.segment_sum(arrived, arrived_place.astype(jnp.int32), num_segments=share_width)
    shares = landed.T
    begin_at = lax.axis_index("state") * share_width
    obs_here = lax.dynamic_slice_in_dim(observed, begin_at, share_width)
    var_here = lax.dynamic_slice_in_dim(inv_var, begin_at, share_width)
    everyone = gather_members(shares)
    gram, pull = statistics(everyone, obs_here, var_here, all_members)
    gram, pull = in_one((gram, pull), "state")
    mixing = transform(gram, pull, all_members)
    regrouped = lax.all_to_all(ensemble, "mem", split_axis=1, concat_axis=0, tiled=True)
    updated = jnp.einsum("jk,js->ks", mixing, regrouped, preferred_element_type=jnp.float32).astype(
        jnp.bfloat16
    )
    return lax.all_to_all(updated, "mem", split_axis=0, concat_axis=1, tiled=True)


def solution(mesh):
    return jax.shard_map(
        per_device,
        mesh=mesh,
        in_specs=(P("mem", "state"), P("state", None, None), P("state", None), P(), P()),
        out_specs=P("mem", "state"),
        check_vma=False,
    )
```

profile of v0, /device:TPU:1, one launch (start us, length us, event | category | flops | bytes accessed | tf_op | source)
XLA Modules:
  0.0 159.3 jit_solution(11215360231634751820)
XLA Ops:
  0.0 0.8 copy.66
  1.0 5.8 %sort.17 = (s32[3072]{0:T(1024)}, s32[3072]{0:T(1024)S(1)}) sort(s32[3072]{0:T(1024)S(1)} %add_select_fusion.1, s32[3072]{0:T(1024)S(1)} %iota.88), dimensions={0}, to_apply=%region_0.1 | sort | flops 36864 | bytes 49152 | tf_op jit(solution)/shard_map/jit(argsort)/sort | solution.py:83
  6.7 17.4 %gather_fusion.1 = s32[3072]{0:T(1024)S(1)} fusion(s32[3072]{0:T(1024)S(1)} %reshape.116, s32[3072]{0:T(1024)S(1)} %fusion.37), kind=kCustom, calls=%fused_computation.1 | custom fusion | bytes 36864 | tf_op jit(solution)/shard_map/gather | solution.py:85
  24.7 1.0 copy-done.2
  25.7 2.7 %fusion = f32[256,12,20]{2,1,0:T(8,128)} fusion(bf16[20,256,128]{2,1,0:T(8,128)(2,1)S(1)} %slice.22, bf16[256,12,128]{2,0,1:T(8,128)(2,1)S(1)} %copy-done.2), kind=kOutput, calls=%fused_computation.4 | convolution fusion | flops 15728640 | bytes 2342912 | tf_op jit(solution)/shard_map/ktc,tjc->tjk/dot_general | solution.py:78
  28.4 1.6 %reshape.154 = f32[3072,20]{1,0:T(8,128)S(1)} reshape(f32[256,12,20]{2,1,0:T(8,128)} %fusion) | data formatting | bytes 491520 | tf_op jit(solution)/shard_map/reshape | solution.py:79
  30.0 8.1 %gather_fusion = f32[3072,20]{1,0:T(8,128)S(1)} fusion(f32[3072,20]{1,0:T(8,128)S(1)} %reshape.154, s32[3072]{0:T(1024)S(1)} %fusion.37), kind=kCustom, calls=%fused_computation | custom fusion | bytes 503808 | tf_op jit(solution)/shard_map/gather | solution.py:84
  38.7 0.8 pad_maximum_fusion
  39.5 8.6 %all-to-all-start = ((f32[32,96,21]{1,2,0:T(8,128)}), f32[32,96,21]{1,2,0:T(8,128)S(1)}, u32[]{:S(2)}, u32[]{:S(2)}) async-start(f32[32,96,21]{1,2,0:T(8,128)} %pad_maximum_fusion), calls=%async_computation | async-start | bytes 786432 | tf_op jit(solution)/shard_map/all_to_all | solution.py:15
  48.1 2.1 %all_to_all.41 = bf16[20,4,8192]{2,1,0:T(4,128)(2,1)S(1)} reshape(bf16[20,32768]{1,0:T(8,128)(2,1)S(1)} %copy-done.1) | data formatting | bytes 2621440 | tf_op jit(solution)/shard_map/all_to_all | solution.py:96
  50.2 1.9 %copy.74 = bf16[20,4,8192]{2,0,1:T(8,128)(2,1)} copy(bf16[20,4,8192]{2,1,0:T(4,128)(2,1)S(1)} %all_to_all.41) | data formatting | bytes 2621440 | tf_op jit(solution)/shard_map/all_to_all | solution.py:96
  52.8 5.6 %all-to-all-done = f32[32,96,21]{1,2,0:T(8,128)S(1)} async-done(((f32[32,96,21]{1,2,0:T(8,128)}), f32[32,96,21]{1,2,0:T(8,128)S(1)}, u32[]{:S(2)}, u32[]{:S(2)}) %all-to-all-start) | async-done | bytes 258080 | tf_op jit(solution)/shard_map/all_to_all | solution.py:15
  58.3 5.0 %all-to-all-start.2 = ((bf16[20,4,8192]{2,0,1:T(8,128)(2,1)}), bf16[20,4,8192]{2,0,1:T(8,128)(2,1)S(1)}, u32[]{:S(2)}, u32[]{:S(2)}) async-start(bf16[20,4,8192]{2,0,1:T(8,128)(2,1)} %copy.74), calls=%async_computation.2 | async-start | bytes 3145728 | tf_op jit(solution)/shard_map/all_to_all | solution.py:96
  63.7 1.7 %copy.71 = f32[3072,20]{1,0:T(8,128)} copy(f32[3072,20]{0,1:T(8,128)S(1)} %bitcast.118) | data formatting | bytes 491520 | tf_op jit(solution)/shard_map/split | solution.py:16
  65.3 17.5 %scatter_custom_fusion = f32[2048,20]{1,0:T(8,128)S(1)} fusion(s32[3072]{0:T(1024)S(1)} %bitcast.121, f32[3072,20]{1,0:T(8,128)} %copy.71, f32[]{:T(128)} %constant.44.clone.1), kind=kCustom, calls=%fused_computation.45 | custom fusion | flops 61440 | bytes 164352 | tf_op jit(solution)/shard_map/scatter-add | solution.py:87
  83.1 10.9 %all-gather = bf16[4,20,2048]{2,1,0:T(8,128)(2,1)S(1)} all-gather(bf16[1,20,2048]{2,1,0:T(8,128)(2,1)S(1)} %copy.72), channel_id=1, replica_groups=mesh['state'=32,'mem'=4] {'mem'}, dimensions={0}, use_global_device_ids=true | all-gather | bytes 409600 | tf_op jit(solution)/shard_map/all_gather | solution.py:67
  96.3 1.3 broadcast_in_dim.8
  97.7 7.1 %all-to-all-start.1 = ((f32[32,1,6480]{2,1,0:T(1,128)}), f32[32,1,6480]{2,1,0:T(1,128)}, u32[]{:S(2)}, u32[]{:S(2)}) async-start(f32[32,1,6480]{2,1,0:T(1,128)} %broadcast_in_dim.8), calls=%async_computation.1 | async-start | bytes 1671168 | tf_op jit(solution)/shard_map/all_to_all | solution.py:22
  105.3 14.4 %all-to-all-done.1 = f32[32,1,6480]{2,1,0:T(1,128)} async-done(((f32[32,1,6480]{2,1,0:T(1,128)}), f32[32,1,6480]{2,1,0:T(1,128)}, u32[]{:S(2)}, u32[]{:S(2)}) %all-to-all-start.1) | async-done | bytes 829472 | tf_op jit(solution)/shard_map/all_to_all | solution.py:22
  119.7 1.6 %reduce_sum.37 = f32[6480]{0:T(1024)S(1)} reduce(f32[32,1,6480]{2,1,0:T(1,128)} %all-to-all-done.1, f32[]{:T(128)} %constant.44.clone.1), dimensions={0,1}, to_apply=%region_3.4 | reduce | flops 200880 | bytes 855364 | tf_op jit(solution)/shard_map/reduce_sum | solution.py:27
  131.5 24.0 %all_to_all.53 = bf16[4,20,8192]{2,1,0:T(8,128)(2,1)S(1)} all-to-all(bf16[4,20,8192]{2,1,0:T(8,128)(2,1)S(1)} %all_to_all.45), channel_id=1, replica_groups=mesh['state'=32,'mem'=4] {'mem'}, dimensions={0} | all-to-all | bytes 2621440 | tf_op jit(solution)/shard_map/all_to_all | solution.py:100
  155.5 1.0 copy.75
  156.6 0.7 pad.6
  157.3 2.0 %copy.81 = bf16[3,8,4,8192]{3,1,2,0:T(8,128)(2,1)} copy(bf16[3,8,4,8192]{3,2,1,0:T(4,128)(2,1)S(1)} %bitcast.113) | data formatting | bytes 3145728
  (80 shorter events, 14.4 us)
Async XLA Ops:
  6.7 17.5 %copy-start = (bf16[20,32768]{1,0:T(8,128)(2,1)S(1)}, bf16[20,32768]{1,0:T(8,128)(2,1)}, u32[]{:S(2)}) copy-start(bf16[20,32768]{1,0:T(8,128)(2,1)} %param.5) | copy-start | bytes 3932164
  24.6 1.1 copy-start.2
  38.2 9.9 %copy-start.1 = (bf16[20,32768]{1,0:T(8,128)(2,1)S(1)}, bf16[20,32768]{1,0:T(8,128)(2,1)}, u32[]{:S(2)}) copy-start(bf16[20,32768]{1,0:T(8,128)(2,1)} %param.5) | copy-start | bytes 3932164
  39.5 18.9 %all-to-all-start = ((f32[32,96,21]{1,2,0:T(8,128)}), f32[32,96,21]{1,2,0:T(8,128)S(1)}, u32[]{:S(2)}, u32[]{:S(2)}) async-start(f32[32,96,21]{1,2,0:T(8,128)} %pad_maximum_fusion), calls=%async_computation | async-start | bytes 786432 | tf_op jit(solution)/shard_map/all_to_all | solution.py:15
  58.3 38.0 %all-to-all-start.2 = ((bf16[20,4,8192]{2,0,1:T(8,128)(2,1)}), bf16[20,4,8192]{2,0,1:T(8,128)(2,1)S(1)}, u32[]{:S(2)}, u32[]{:S(2)}) async-start(bf16[20,4,8192]{2,0,1:T(8,128)(2,1)} %copy.74), calls=%async_computation.2 | async-start | bytes 3145728 | tf_op jit(solution)/shard_map/all_to_all | solution.py:96
  97.7 22.0 %all-to-all-start.1 = ((f32[32,1,6480]{2,1,0:T(1,128)}), f32[32,1,6480]{2,1,0:T(1,128)}, u32[]{:S(2)}, u32[]{:S(2)}) async-start(f32[32,1,6480]{2,1,0:T(1,128)} %broadcast_in_dim.8), calls=%async_computation.1 | async-start | bytes 1671168 | tf_op jit(solution)/shard_map/all_to_all | solution.py:22
where the time goes:
time: 160 us; the launch traced here: 159 us
  local copies, waits for them, and re-layouts  43.1 us (27%)
  blocking collectives  34.9 us (22%)
  other arithmetic  27.3 us (17%)
  starting transfers between devices  20.7 us (13%)
  waiting for transfers between devices  20 us (12%)
  matrix products  11.9 us (7%)
    all_to_all x1, blocking collectives, per_device(): lax.all_to_all(updated, 'mem', split_axis=0, concat_axis=1, tiled=True)  24 us
    scatter-add x1, other arithmetic, per_device(): jax.ops.segment_sum(arrived, arrived_place.astype(jnp.int32), num_segment...  17.5 us
    gather x2, local copies, waits for them, and re-layouts, per_device(): local_place = (slot_ids[order] % share_width).astype(jnp.float32)  17.5 us
    all_to_all x1, waiting for transfers between devices, copy_for_each(): lax.all_to_all(jnp.broadcast_to(x[None], (peers, *x.shape)), axis, 0, 0,...  14.4 us
    all_gather x1, blocking collectives, gather_members(): lax.all_gather(shares.astype(jnp.bfloat16), 'mem', axis=0, tiled=True)  10.9 us
    all_to_all x1, starting transfers between devices, sent_together(): lax.all_to_all(both, axis, split_axis=split_dim, concat_axis=concat_dim,...  8.57 us
    gather x1, local copies, waits for them, and re-layouts, per_device(): sorted_values = values[order]  8.12 us
    all_to_all x1, starting transfers between devices, copy_for_each(): lax.all_to_all(jnp.broadcast_to(x[None], (peers, *x.shape)), axis, 0, 0,...  7.1 us
  transfers between devices with their start and end apart: 3, of which 2 were waited for; matrix products, arithmetic and copies ran while one was open for 15% of the time, Pallas kernels for 0%

commit v1 on v0

--- a/solution.py
+++ b/solution.py
@@ -5,6 +5,28 @@
 from jax.sharding import PartitionSpec as P
 
 ITERS = 14
+
+
+def in_order(blocks, dim):
+    blocks = jnp.moveaxis(blocks, 0, dim)
+    dims = blocks.shape
+    return blocks.reshape(*dims[:dim], dims[dim] * dims[dim + 1], *dims[dim + 2 :])
+
+
+def collect(x, axis, dim):
+    length = lax.axis_size(axis)
+    pairs = [(i, (i + 1) % length) for i in range(length)]
+    back = [(b, a) for a, b in pairs]
+    lower, upper = ([], [])
+    for step in range(length - 1):
+        if step % 2 == 0:
+            lower.append(lax.ppermute(lower[-1] if lower else x, axis, pairs))
+        else:
+            upper.append(lax.ppermute(upper[-1] if upper else x, axis, back))
+    tiles = jnp.stack([*lower[::-1], x, *upper])
+    shift = lax.axis_index(axis) - len(lower)
+    tiles = tiles[(jnp.arange(length) - shift) % length]
+    return in_order(tiles, dim)
 
 
 def sent_together(arrays, axis, split_dim, concat_dim, along):
@@ -64,9 +86,7 @@
 
 
 def gather_members(shares):
-    return lax.all_gather(shares.astype(jnp.bfloat16), "mem", axis=0, tiled=True).astype(
-        jnp.float32
-    )
+    return collect(shares.astype(jnp.bfloat16), "mem", 0).astype(jnp.float32)
 
 
 def per_device(ensemble, weights, seg_obs, observed, inv_var):

time: 160 us -> 175 us (1.094)
  waiting for transfers between devices: 20 us -> 44.9 us
  blocking collectives: 34.9 us -> 23.1 us
    ppermute x0 -> x3, waiting for transfers between devices: none -> 26.2 us  [the longest x2 26.2 us: collect(): lower.append(lax.ppermute(lower[-1] if lower else x, axis, pairs))]
    all_gather x1 -> x0, blocking collectives: 10.9 us -> none  [gather_members(): lax.all_gather(shares.astype(jnp.bfloat16), 'mem', axis=0, tiled=True)]
    ppermute x0 -> x3, starting transfers between devices: none -> 3.26 us  [the longest x1 1.73 us: collect(): upper.append(lax.ppermute(upper[-1] if upper else x, axis, back))]
    all_to_all x1, starting transfers between devices: 7.1 us -> 5.05 us  [copy_for_each(): lax.all_to_all(jnp.broadcast_to(x[None], (peers, *x.shape)), axis, 0, 0,...]
    unnamed x11 -> x10, local copies, waits for them, and re-layouts: 5.16 us -> 4.93 us
  transfers between devices with their start and end apart: 3 -> 6, of which waited for: 2 -> 4; matrix products, arithmetic and copies ran while one was open for 15% -> 14% of each run, Pallas kernels for 0% -> 0%
where the time goes in v1:
time: 175 us; the launch traced here: 174 us
  waiting for transfers between devices  44.9 us (26%)
  local copies, waits for them, and re-layouts  44.6 us (25%)
  other arithmetic  26.7 us (15%)
  blocking collectives  23.1 us (13%)
  starting transfers between devices  21.9 us (13%)
  matrix products  11.9 us (7%)
    ppermute x2, waiting for transfers between devices, collect(): lower.append(lax.ppermute(lower[-1] if lower else x, axis, pairs))  26.2 us
    all_to_all x1, blocking collectives, per_device(): lax.all_to_all(updated, 'mem', split_axis=0, concat_axis=1, tiled=True)  23.1 us
    gather x2, local copies, waits for them, and re-layouts, per_device(): local_place = (slot_ids[order] % share_width).astype(jnp.float32)  17.5 us
    scatter-add x1, other arithmetic, per_device(): jax.ops.segment_sum(arrived, arrived_place.astype(jnp.int32), num_segment...  17.2 us
    all_to_all x1, waiting for transfers between devices, copy_for_each(): lax.all_to_all(jnp.broadcast_to(x[None], (peers, *x.shape)), axis, 0, 0,...  13.2 us
    all_to_all x1, starting transfers between devices, sent_together(): lax.all_to_all(both, axis, split_axis=split_dim, concat_axis=concat_dim,...  8.57 us
    gather x1, local copies, waits for them, and re-layouts, per_device(): sorted_values = values[order]  8.12 us
    sort x1, other arithmetic, per_device(): order = jnp.argsort(owner, stable=True)  5.76 us
  transfers between devices with their start and end apart: 6, of which 4 were waited for; matrix products, arithmetic and copies ran while one was open for 14% of the time, Pallas kernels for 0%

profile of v1, /device:TPU:1, one launch (start us, length us, event | category | flops | bytes accessed | tf_op | source)
XLA Modules:
  0.0 174.4 jit_solution(4677313290568435795)
XLA Ops:
  1.0 5.8 %sort.17 = (s32[3072]{0:T(1024)}, s32[3072]{0:T(1024)S(1)}) sort(s32[3072]{0:T(1024)S(1)} %add_select_fusion.1, s32[3072]{0:T(1024)S(1)} %iota.92), dimensions={0}, to_apply=%region_0.1 | sort | flops 36864 | bytes 49152 | tf_op jit(solution)/shard_map/jit(argsort)/sort | solution.py:103
  6.7 17.4 %gather_fusion.1 = s32[3072]{0:T(1024)S(1)} fusion(s32[3072]{0:T(1024)S(1)} %reshape.233, s32[3072]{0:T(1024)S(1)} %fusion.32), kind=kCustom, calls=%fused_computation.1 | custom fusion | bytes 36864 | tf_op jit(solution)/shard_map/gather | solution.py:105
  24.7 1.0 copy-done.2
  25.7 2.7 %fusion = f32[256,12,20]{2,1,0:T(8,128)} fusion(bf16[20,256,128]{2,1,0:T(8,128)(2,1)S(1)} %slice.24, bf16[256,12,128]{2,0,1:T(8,128)(2,1)S(1)} %copy-done.2), kind=kOutput, calls=%fused_computation.6 | convolution fusion | flops 15728640 | bytes 2342912 | tf_op jit(solution)/shard_map/ktc,tjc->tjk/dot_general | solution.py:98
  28.4 1.6 reshape.277
  30.0 8.1 %gather_fusion = f32[3072,20]{1,0:T(8,128)S(1)} fusion(f32[3072,20]{1,0:T(8,128)S(1)} %reshape.277, s32[3072]{0:T(1024)S(1)} %fusion.32), kind=kCustom, calls=%fused_computation | custom fusion | bytes 503808 | tf_op jit(solution)/shard_map/gather | solution.py:104
  39.5 8.6 %all-to-all-start = ((f32[32,96,21]{1,2,0:T(8,128)}), f32[32,96,21]{1,2,0:T(8,128)S(1)}, u32[]{:S(2)}, u32[]{:S(2)}) async-start(f32[32,96,21]{1,2,0:T(8,128)} %pad_maximum_fusion.1), calls=%async_computation | async-start | bytes 786432 | tf_op jit(solution)/shard_map/all_to_all | solution.py:37
  48.1 2.1 %all_to_all.41 = bf16[20,4,8192]{2,1,0:T(4,128)(2,1)S(1)} reshape(bf16[20,32768]{1,0:T(8,128)(2,1)S(1)} %copy-done.1) | data formatting | bytes 2621440 | tf_op jit(solution)/shard_map/all_to_all | solution.py:116
  50.2 1.9 %copy.82 = bf16[20,4,8192]{2,0,1:T(8,128)(2,1)} copy(bf16[20,4,8192]{2,1,0:T(4,128)(2,1)S(1)} %all_to_all.41) | data formatting | bytes 2621440 | tf_op jit(solution)/shard_map/all_to_all | solution.py:116
  52.8 5.6 %all-to-all-done = f32[32,96,21]{1,2,0:T(8,128)S(1)} async-done(((f32[32,96,21]{1,2,0:T(8,128)}), f32[32,96,21]{1,2,0:T(8,128)S(1)}, u32[]{:S(2)}, u32[]{:S(2)}) %all-to-all-start) | async-done | bytes 258080 | tf_op jit(solution)/shard_map/all_to_all | solution.py:37
  58.3 5.0 %all-to-all-start.2 = ((bf16[20,4,8192]{2,0,1:T(8,128)(2,1)}), bf16[20,4,8192]{2,0,1:T(8,128)(2,1)}, u32[]{:S(2)}, u32[]{:S(2)}) async-start(bf16[20,4,8192]{2,0,1:T(8,128)(2,1)} %copy.82), calls=%async_computation.2 | async-start | bytes 3145728 | tf_op jit(solution)/shard_map/all_to_all | solution.py:116
  64.2 17.2 %scatter_custom_fusion = f32[2048,20]{1,0:T(8,128)S(1)} fusion(s32[3072]{0:T(1024)S(1)} %bitcast.131, f32[3072,20]{1,0:T(8,128)S(1)} %copy.79, f32[]{:T(128)} %constant.62.clone.1), kind=kCustom, calls=%fused_computation.43 | custom fusion | flops 61440 | bytes 163844 | tf_op jit(solution)/shard_map/scatter-add | solution.py:107
  81.5 1.5 collective-permute-start
  83.1 1.7 collective-permute-start.2
  84.8 12.1 %collective-permute-done = bf16[20,2048]{0,1:T(8,128)(2,1)S(1)} collective-permute-done((bf16[20,2048]{0,1:T(8,128)(2,1)S(1)}, bf16[20,2048]{0,1:T(8,128)(2,1)S(1)}, u32[]{:S(2)}, u32[]{:S(2)}) %collective-permute-start) | collective-permute-done | bytes 81952 | tf_op jit(solution)/shard_map/ppermute | solution.py:23
  97.0 14.0 %collective-permute-done.1 = bf16[20,2048]{0,1:T(8,128)(2,1)S(1)} collective-permute-done((bf16[20,2048]{0,1:T(8,128)(2,1)S(1)}, bf16[20,2048]{0,1:T(8,128)(2,1)S(1)}, u32[]{:S(2)}, u32[]{:S(2)}) %collective-permute-start.1) | collective-permute-done | bytes 81952 | tf_op jit(solution)/shard_map/ppermute | solution.py:23
  111.5 0.9 copy.80
  115.7 1.3 broadcast_in_dim.8
  117.0 5.1 %all-to-all-start.1 = ((f32[32,1,6480]{2,1,0:T(1,128)}), f32[32,1,6480]{2,1,0:T(1,128)S(1)}, u32[]{:S(2)}, u32[]{:S(2)}) async-start(f32[32,1,6480]{2,1,0:T(1,128)} %broadcast_in_dim.8), calls=%async_computation.1 | async-start | bytes 1671168 | tf_op jit(solution)/shard_map/all_to_all | solution.py:44
  122.2 1.6 all_to_all.44
  123.8 13.2 %all-to-all-done.1 = f32[32,1,6480]{2,1,0:T(1,128)S(1)} async-done(((f32[32,1,6480]{2,1,0:T(1,128)}), f32[32,1,6480]{2,1,0:T(1,128)S(1)}, u32[]{:S(2)}, u32[]{:S(2)}) %all-to-all-start.1) | async-done | bytes 829472 | tf_op jit(solution)/shard_map/all_to_all | solution.py:44
  147.6 23.1 %all_to_all.53 = bf16[4,20,8192]{2,1,0:T(8,128)(2,1)S(1)} all-to-all(bf16[4,20,8192]{2,1,0:T(8,128)(2,1)S(1)} %all_to_all.45), channel_id=1, replica_groups=mesh['state'=32,'mem'=4] {'mem'}, dimensions={0} | all-to-all | bytes 2621440 | tf_op jit(solution)/shard_map/all_to_all | solution.py:120
  170.7 1.0 copy.83
  172.4 2.0 %copy.89 = bf16[3,8,4,8192]{3,1,2,0:T(8,128)(2,1)} copy(bf16[3,8,4,8192]{3,2,1,0:T(4,128)(2,1)S(1)} %bitcast.121) | data formatting | bytes 3145728
  (92 shorter events, 18.6 us)
Async XLA Ops:
  6.7 17.5 %copy-start = (bf16[20,32768]{1,0:T(8,128)(2,1)S(1)}, bf16[20,32768]{1,0:T(8,128)(2,1)}, u32[]{:S(2)}) copy-start(bf16[20,32768]{1,0:T(8,128)(2,1)} %param.5) | copy-start | bytes 3932164
  24.6 1.1 copy-start.2
  38.2 9.9 %copy-start.1 = (bf16[20,32768]{1,0:T(8,128)(2,1)S(1)}, bf16[20,32768]{1,0:T(8,128)(2,1)}, u32[]{:S(2)}) copy-start(bf16[20,32768]{1,0:T(8,128)(2,1)} %param.5) | copy-start | bytes 3932164
  39.5 18.9 %all-to-all-start = ((f32[32,96,21]{1,2,0:T(8,128)}), f32[32,96,21]{1,2,0:T(8,128)S(1)}, u32[]{:S(2)}, u32[]{:S(2)}) async-start(f32[32,96,21]{1,2,0:T(8,128)} %pad_maximum_fusion.1), calls=%async_computation | async-start | bytes 786432 | tf_op jit(solution)/shard_map/all_to_all | solution.py:37
  58.3 57.4 %all-to-all-start.2 = ((bf16[20,4,8192]{2,0,1:T(8,128)(2,1)}), bf16[20,4,8192]{2,0,1:T(8,128)(2,1)}, u32[]{:S(2)}, u32[]{:S(2)}) async-start(bf16[20,4,8192]{2,0,1:T(8,128)(2,1)} %copy.82), calls=%async_computation.2 | async-start | bytes 3145728 | tf_op jit(solution)/shard_map/all_to_all | solution.py:116
  81.5 15.4 %collective-permute-start = (bf16[20,2048]{0,1:T(8,128)(2,1)S(1)}, bf16[20,2048]{0,1:T(8,128)(2,1)S(1)}, u32[]{:S(2)}, u32[]{:S(2)}) collective-permute-start(bf16[20,2048]{0,1:T(8,128)(2,1)S(1)} %get-tuple-element.8), channel_id=1, source_target_pairs={{0,1},{1,2},{2,3},{3,0},{4,5},{5,6},{6,7},{7,4},{8,9},{9,10},{10,1... | collective-permute-start | bytes 245768 | tf_op jit(solution)/shard_map/ppermute | solution.py:23
  83.1 13.9 %collective-permute-start.2 = (bf16[20,2048]{0,1:T(8,128)(2,1)S(1)}, bf16[20,2048]{0,1:T(8,128)(2,1)S(1)}, u32[]{:S(2)}, u32[]{:S(2)}) collective-permute-start(bf16[20,2048]{0,1:T(8,128)(2,1)S(1)} %get-tuple-element.8), channel_id=1, source_target_pairs={{1,0},{2,1},{3,2},{0,3},{5,4},{6,5},{7,6},{4,7},{9,8},{10,9},{11,1... | collective-permute-start | bytes 245768 | tf_op jit(solution)/shard_map/ppermute | solution.py:25
  96.9 14.1 %collective-permute-start.1 = (bf16[20,2048]{0,1:T(8,128)(2,1)S(1)}, bf16[20,2048]{0,1:T(8,128)(2,1)S(1)}, u32[]{:S(2)}, u32[]{:S(2)}) collective-permute-start(bf16[20,2048]{0,1:T(8,128)(2,1)S(1)} %collective-permute-done), channel_id=1, source_target_pairs={{0,1},{1,2},{2,3},{3,0},{4,5},{5,6},{6,7},{7,4},{8,9},{9,10},{10,1... | collective-permute-start | bytes 245768 | tf_op jit(solution)/shard_map/ppermute | solution.py:23
  117.0 19.9 %all-to-all-start.1 = ((f32[32,1,6480]{2,1,0:T(1,128)}), f32[32,1,6480]{2,1,0:T(1,128)S(1)}, u32[]{:S(2)}, u32[]{:S(2)}) async-start(f32[32,1,6480]{2,1,0:T(1,128)} %broadcast_in_dim.8), calls=%async_computation.1 | async-start | bytes 1671168 | tf_op jit(solution)/shard_map/all_to_all | solution.py:44
